TPU v7x, 512 devices: a whole 4x4x16 slice. The times are simulated.
512 devices in a mesh: row: 16 (over z_lo, y), mode: 32 (over z_hi, x, core).
Axes of the slice: x: 4, y: 4, z: 16 (z_hi: 4, z_lo: 4; z = z_hi * 4 + z_lo), core: 2. Of those that a mesh axis runs over, the one named last changes fastest.
Arguments:
- transfer_matrix: float32 [2, 3072, 49152], P(None, 'row', 'mode'), may hold values from -0.01953125 to 0.01953125
- probes: float32 [2, 49152, 256], P(None, ('mode', 'row')), may hold values from -6 to 6
- intensity: float32 [3072, 256], P('row'), may hold values from 0.25 to 4
Outputs:
- gradient: float32 [2, 3072, 49152], P(None, 'row', 'mode')
All inputs are finite; a program needn't handle non-finite values.
Results may differ from a plain program's by a relative error of at most 0.00012.
Values sent between devices are 32-bit elements; how exact they have to be, the bound alone decides.
A program may use at most 64 MiB of HBM per device.

v0:
```python
import jax
import jax.numpy as jnp
from jax import lax
from jax.sharding import Mesh
from jax.sharding import PartitionSpec as P

P_SIZE = 256
ROW = ("row_0", "row_1")
MODE_ROW = ("mode", "row_0", "row_1")


def joined_along(tiles, dim):
    lengths = list(tiles.shape[1:])
    lengths[dim] *= tiles.shape[0]
    return jnp.moveaxis(tiles, 0, dim).reshape(lengths)


def stacked_from(array, axes, turns):
    tiles = array[None]
    for k in turns:
        tiles = lax.all_gather(tiles, axes[k], axis=0, tiled=True)
    block = [lax.axis_size(axes[k]) for k in reversed(turns)]
    tiles = tiles.reshape(*block, *array.shape)
    turned = sorted(range(len(turns)), key=lambda place: turns[len(turns) - 1 - place])
    return tiles.transpose(*turned, *range(len(turns), tiles.ndim)).reshape(-1, *array.shape)


def whole_of(array, axes, turns, dim):
    return joined_along(stacked_from(array, axes, turns), dim)


def split_up(array, dim, count):
    before, after = (array.shape[:dim], array.shape[dim + 1 :])
    return jnp.moveaxis(array.reshape(*before, count, -1, *after), dim, 0)


def sum_at_owner(array, axis, dim):
    count = lax.axis_size(axis)
    tiles = lax.all_to_all(split_up(array, dim, count), axis, 0, 0, tiled=True)
    return jnp.sum(tiles, axis=0)


def sent_to_all(array, axis):
    count = lax.axis_size(axis)
    return lax.all_to_all(
        jnp.broadcast_to(array[None], (count, *array.shape)), axis, 0, 0, tiled=True
    )


def gather_directly(array, axis, dim):
    tiles = sent_to_all(array, axis)
    return joined_along(tiles, dim)


def exact_dot(left, right):
    return jnp.dot(left, right, precision=lax.Precision.HIGHEST, preferred_element_type=jnp.float32)


def exact_dot_transposed(left, right):
    return lax.dot_general(
        left,
        right,
        (((1,), (1,)), ((), ())),
        precision=lax.Precision.HIGHEST,
        preferred_element_type=jnp.float32,
    )


def partial_fields(matrix, strip):
    fields_real = exact_dot(matrix[0], strip[0]) - exact_dot(matrix[1], strip[1])
    fields_imag = exact_dot(matrix[0], strip[1]) + exact_dot(matrix[1], strip[0])
    return jnp.stack([fields_real, fields_imag])


def gradient_columns(residual, strip):
    grad_real = exact_dot_transposed(residual[0], strip[0]) + exact_dot_transposed(
        residual[1], strip[1]
    )
    grad_imag = exact_dot_transposed(residual[1], strip[0]) - exact_dot_transposed(
        residual[0], strip[1]
    )
    return jnp.stack([grad_real, grad_imag])


def make_residual(fields, measured):
    excess = fields[0] * fields[0] + fields[1] * fields[1] - measured
    return excess[None] * fields / P_SIZE


def body(transfer_matrix, probes, intensity):
    strip = whole_of(probes, ROW, (0, 1), 1)
    partial_value = partial_fields(transfer_matrix, strip)
    shares = sum_at_owner(partial_value, "mode", 2)
    share_width = shares.shape[2]
    measured = lax.dynamic_slice_in_dim(
        intensity, lax.axis_index("mode") * share_width, share_width, 1
    )
    residual = gather_directly(make_residual(shares, measured), "mode", 2)
    return gradient_columns(residual, strip)


def solution(mesh):
    split = Mesh(mesh.devices.reshape(4, 4, mesh.shape["mode"]), ("row_0", "row_1", "mode"))
    placed = (P(None, ROW, "mode"), P(None, MODE_ROW, None), P(ROW, None))
    return jax.shard_map(
        body, mesh=split, in_specs=placed, out_specs=P(None, ROW, "mode"), check_vma=False
    )
```

profile of v0, /device:TPU:38, one launch (start us, length us, event | category | flops | bytes accessed | tf_op | source)
XLA Modules:
  0.0 200.2 jit_solution(12416556249650519281)
XLA Ops:
  6.5 0.0 copy-start
  6.5 0.0 all-gather.3.cloned.1.call-start
  6.5 20.1 %all-gather = f32[8,96,256]{2,1,0:T(8,128)} all-gather(f32[2,96,256]{2,1,0:T(8,128)} %param.4), channel_id=2, replica_groups=mesh['row_0'=4,'row_1'=4,'mode'=32] {'row_0'}, dimensions={0}, use_global_device_ids=true | all-gather | bytes 983040 | tf_op jit(solution)/shard_map/all_gather | solution.py:21
  26.6 0.0 all-gather.3.cloned.1.call-update
  26.6 50.7 %all-gather.3.cloned.1.call-done = f32[16,2,96,256]{3,2,1,0:T(8,128)} async-done(((f32[4,2,96,256]{3,2,1,0:T(8,128)}), f32[16,2,96,256]{3,2,1,0:T(8,128)}) %all-gather.3.cloned.1.call-update) | async-done | bytes 3145744 | tf_op jit(solution)/shard_map/all_gather | solution.py:21
  77.4 2.2 %copy.11 = f32[4,4,2,96,256]{4,3,2,1,0:T(8,128)S(1)} copy(f32[4,4,2,96,256]{4,3,2,0,1:T(8,128)} %bitcast.65) | data formatting | bytes 6291456 | tf_op jit(solution)/shard_map/transpose | solution.py:25
  79.6 0.0 copy-start.1
  79.6 0.3 fusion.25
  80.0 1.3 copy-done.1
  81.3 1.2 fusion.4
  82.5 1.2 fusion.2
  83.7 1.9 fusion.10
  85.6 1.8 copy.12
  87.3 3.1 %fusion.13 = f32[192,256]{1,0:T(8,128)} fusion(f32[192,256]{1,0:T(8,128)S(1)} %fusion.2, f32[1536,256]{1,0:T(8,128)S(1)} %bitcast.57, f32[2,192,1536]{2,1,0:T(8,128)} %param.3), kind=kOutput, calls=%fused_computation.14 | convolution fusion | flops 906018816 | bytes 3145728 | tf_op jit(solution)/shard_map/dot_general | solution.py:56
  90.5 1.8 copy.13
  92.2 1.1 maximum_bitcast_fusion
  93.3 0.9 copy.14
  94.1 14.5 %all-to-all-start = ((f32[32,2,192,8]{2,3,1,0:T(8,128)}), f32[32,2,192,8]{2,3,1,0:T(8,128)}, u32[]{:S(2)}, u32[]{:S(2)}) async-start(f32[32,2,192,8]{2,3,1,0:T(8,128)} %copy.14), calls=%async_computation | async-start | bytes 1048576 | tf_op jit(solution)/shard_map/all_to_all | solution.py:39
  108.6 0.0 copy-done
  108.6 0.1 constant_dynamic-slice_fusion
  108.7 0.1 copy.18
  108.8 33.0 %all-to-all-done = f32[32,2,192,8]{2,3,1,0:T(8,128)} async-done(((f32[32,2,192,8]{2,3,1,0:T(8,128)}), f32[32,2,192,8]{2,3,1,0:T(8,128)}, u32[]{:S(2)}, u32[]{:S(2)}) %all-to-all-start) | async-done | bytes 393248 | tf_op jit(solution)/shard_map/all_to_all | solution.py:39
  141.7 1.1 reduce_sum.9
  142.9 0.1 broadcast_in_dim.5
  142.9 38.2 %all_to_all.10 = f32[32,2,192,8]{2,3,1,0:T(8,128)S(1)} all-to-all(f32[32,2,192,8]{2,3,1,0:T(8,128)S(1)} %broadcast_in_dim.5), channel_id=1, replica_groups=mesh['row_0'=4,'row_1'=4,'mode'=32] {'mode'}, dimensions={0} | all-to-all | bytes 786432 | tf_op jit(solution)/shard_map/all_to_all | solution.py:45
  181.1 2.7 %fusion.20 = f32[192,1536]{1,0:T(8,128)S(1)} fusion(f32[1536,256]{1,0:T(8,128)S(1)} %bitcast.54, f32[2,192,32,8]{1,3,0,2:T(8,128)S(1)} %bitcast.61), kind=kOutput, calls=%fused_computation.22 | convolution fusion | flops 905969664 | bytes 3014656 | tf_op jit(solution)/shard_map/dot_general | solution.py:60
  183.8 2.7 %fusion.21 = f32[192,1536]{1,0:T(8,128)S(1)} fusion(f32[1536,256]{1,0:T(8,128)S(1)} %bitcast.55, f32[2,192,32,8]{1,3,0,2:T(8,128)S(1)} %bitcast.62), kind=kOutput, calls=%fused_computation.23 | convolution fusion | flops 905969664 | bytes 3014656 | tf_op jit(solution)/shard_map/dot_general | solution.py:60
  186.5 2.7 %fusion = f32[1,192,1536]{2,1,0:T(8,128)S(1)} fusion(f32[192,1536]{1,0:T(8,128)S(1)} %fusion.20, f32[1536,256]{1,0:T(8,128)S(1)} %bitcast.58, f32[2,192,32,8]{1,3,0,2:T(8,128)S(1)} %bitcast.63), kind=kOutput, calls=%fused_computation.2 | convolution fusion | flops 906264576 | bytes 4194304 | tf_op jit(solution)/shard_map/dot_general | solution.py:60
  189.1 2.7 %fusion.1 = f32[1,192,1536]{2,1,0:T(8,128)S(1)} fusion(f32[192,1536]{1,0:T(8,128)S(1)} %fusion.21, f32[1536,256]{1,0:T(8,128)S(1)} %bitcast.59, f32[2,192,32,8]{1,3,0,2:T(8,128)S(1)} %bitcast.64), kind=kOutput, calls=%fused_computation.3 | convolution fusion | flops 906264576 | bytes 4194304 | tf_op jit(solution)/shard_map/dot_general | solution.py:60
  191.8 1.6 pad_maximum_fusion
  (2 shorter events, 0.0 us)
Async XLA Ops:
  6.5 102.1 %copy-start = (f32[192,256]{1,0:T(8,128)S(1)}, f32[192,256]{1,0:T(8,128)}, u32[]{:S(2)}) copy-start(f32[192,256]{1,0:T(8,128)} %param.5) | copy-start | bytes 589828
  6.5 70.8 %all-gather.3.cloned.1.call-start = ((), (), s32[]{:S(2)}) async-start(), calls=%async_computation.2 | async-start | bytes 3932160 | tf_op jit(solution)/shard_map/all_gather | solution.py:21
  79.6 1.7 copy-start.1
  94.1 47.6 %all-to-all-start = ((f32[32,2,192,8]{2,3,1,0:T(8,128)}), f32[32,2,192,8]{2,3,1,0:T(8,128)}, u32[]{:S(2)}, u32[]{:S(2)}) async-start(f32[32,2,192,8]{2,3,1,0:T(8,128)} %copy.14), calls=%async_computation | async-start | bytes 1048576 | tf_op jit(solution)/shard_map/all_to_all | solution.py:39
Sparse Core Ops, SparseCore 0:
  26.8 50.5 all-gather.2
where the time goes:
time: 201 us; the launch traced here: 200 us
  waiting for transfers between devices  83.7 us (42%)
  blocking collectives  58.3 us (29%)
  matrix products  18.1 us (9%)
  starting transfers between devices  14.5 us (7%)
  between operations  13.5 us (7%)
  local copies, waits for them, and re-layouts  8.45 us (4%)
  other arithmetic  3.73 us (2%)
    all_gather x1, waiting for transfers between devices, stacked_from(): tiles = lax.all_gather(tiles, axes[k], axis=0, tiled=True)  50.7 us
    all_to_all x1, blocking collectives, sent_to_all(): lax.all_to_all(jnp.broadcast_to(array[None], (count, *array.shape)), axis...  38.2 us
    all_to_all x1, waiting for transfers between devices, sum_at_owner(): tiles = lax.all_to_all(split_up(array, dim, count), axis, 0, 0, tiled=True)  33 us
    all_gather x1, blocking collectives, stacked_from(): tiles = lax.all_gather(tiles, axes[k], axis=0, tiled=True)  20.1 us
    all_to_all x1, starting transfers between devices, sum_at_owner(): tiles = lax.all_to_all(split_up(array, dim, count), axis, 0, 0, tiled=True)  14.5 us
    dot_general x4, matrix products, exact_dot_transposed(): lax.dot_general(left, right, (((1,), (1,)), ((), ())), precision=lax.Prec...  10.7 us
    dot_general x4, matrix products, exact_dot(): jnp.dot(left, right, precision=lax.Precision.HIGHEST, preferred_element_t...  7.41 us
  transfers between devices with their start and end apart: 2, of which 2 were waited for; matrix products, arithmetic and copies ran while one was open for 0% of the time, Pallas kernels for 0%

commit v1 on v0

--- a/solution.py
+++ b/solution.py
@@ -18,7 +18,10 @@
 def stacked_from(array, axes, turns):
     tiles = array[None]
     for k in turns:
-        tiles = lax.all_gather(tiles, axes[k], axis=0, tiled=True)
+        size = lax.axis_size(axes[k])
+        blocks = jnp.stack([tiles for _ in range(size)])
+        blocks = lax.all_to_all(blocks, axes[k], split_axis=0, concat_axis=0)
+        tiles = jnp.concatenate(blocks, axis=0)
     block = [lax.axis_size(axes[k]) for k in reversed(turns)]
     tiles = tiles.reshape(*block, *array.shape)
     turned = sorted(range(len(turns)), key=lambda place: turns[len(turns) - 1 - place])

time: 201 us -> 183 us (0.910)
  the two profiles are of different devices: /device:TPU:38 before, /device:TPU:36 now
where the time goes in v1:
time: 183 us; the launch traced here: 182 us
  blocking collectives  104 us (57%)
  waiting for transfers between devices  32.8 us (18%)
  matrix products  18.1 us (10%)
  starting transfers between devices  15.6 us (9%)
  local copies, waits for them, and re-layouts  7.93 us (4%)
  other arithmetic  3.73 us (2%)
    all_to_all x2, blocking collectives, stacked_from(): blocks = lax.all_to_all(blocks, axes[k], split_axis=0, concat_axis=0)  64.5 us
    all_to_all x1, blocking collectives, sent_to_all(): lax.all_to_all(jnp.broadcast_to(array[None], (count, *array.shape)), axis...  39.3 us
    all_to_all x1, waiting for transfers between devices, sum_at_owner(): tiles = lax.all_to_all(split_up(array, dim, count), axis, 0, 0, tiled=True)  32.8 us
    all_to_all x1, starting transfers between devices, sum_at_owner(): tiles = lax.all_to_all(split_up(array, dim, count), axis, 0, 0, tiled=True)  15.6 us
    dot_general x4, matrix products, exact_dot_transposed(): lax.dot_general(left, right, (((1,), (1,)), ((), ())), precision=lax.Prec...  10.7 us
    dot_general x4, matrix products, exact_dot(): jnp.dot(left, right, precision=lax.Precision.HIGHEST, preferred_element_t...  7.44 us
  transfers between devices with their start and end apart: 1, of which 1 were waited for; matrix products, arithmetic and copies ran while one was open for 0% of the time, Pallas kernels for 0%

profile of v1, /device:TPU:36, one launch (start us, length us, event | category | flops | bytes accessed | tf_op | source)
XLA Modules:
  0.0 182.1 jit_solution(3771720269124647582)
XLA Ops:
  0.0 0.0 copy-start
  0.0 1.0 stack.24
  1.0 24.1 %all_to_all.20 = f32[4,1,2,96,256]{4,3,2,1,0:T(8,128)S(1)} all-to-all(f32[4,1,2,96,256]{4,3,2,1,0:T(8,128)S(1)} %stack.24), channel_id=1, replica_groups=mesh['row_0'=4,'row_1'=4,'mode'=32] {'row_0'}, dimensions={0} | all-to-all | bytes 1572864 | tf_op jit(solution)/shard_map/all_to_all | solution.py:23
  25.1 0.4 stack.25
  25.5 40.4 %all_to_all.21 = f32[4,4,2,96,256]{4,3,2,1,0:T(8,128)S(1)} all-to-all(f32[4,4,2,96,256]{4,3,2,1,0:T(8,128)S(1)} %stack.25), channel_id=1, replica_groups=mesh['row_0'=4,'row_1'=4,'mode'=32] {'row_1'}, dimensions={0} | all-to-all | bytes 6291456 | tf_op jit(solution)/shard_map/all_to_all | solution.py:23
  65.9 0.3 copy.7
  66.2 0.0 copy-start.1
  66.2 0.3 fusion.25
  66.6 1.3 copy-done.1
  67.9 1.2 fusion.4
  69.1 1.2 fusion.2
  70.3 1.9 %fusion.10 = f32[192,256]{1,0:T(8,128)} fusion(f32[192,256]{1,0:T(8,128)S(1)} %fusion.4, f32[1536,256]{1,0:T(8,128)S(1)} %bitcast.52, f32[2,192,1536]{2,1,0:T(8,128)S(1)} %copy-done.1), kind=kOutput, calls=%fused_computation.13 | convolution fusion | flops 906018816 | bytes 3145728 | tf_op jit(solution)/shard_map/dot_general | solution.py:59
  72.2 1.7 copy.8
  74.0 3.1 %fusion.13 = f32[192,256]{1,0:T(8,128)} fusion(f32[192,256]{1,0:T(8,128)S(1)} %fusion.2, f32[1536,256]{1,0:T(8,128)S(1)} %bitcast.56, f32[2,192,1536]{2,1,0:T(8,128)} %param.3), kind=kOutput, calls=%fused_computation.14 | convolution fusion | flops 906018816 | bytes 3145728 | tf_op jit(solution)/shard_map/dot_general | solution.py:59
  77.1 1.8 copy.9
  78.9 1.1 maximum_bitcast_fusion
  79.9 0.9 copy.10
  80.8 15.6 %all-to-all-start.2 = ((f32[32,2,192,8]{2,3,1,0:T(8,128)}), f32[32,2,192,8]{2,3,1,0:T(8,128)}, u32[]{:S(2)}, u32[]{:S(2)}) async-start(f32[32,2,192,8]{2,3,1,0:T(8,128)} %copy.10), calls=%async_computation.2 | async-start | bytes 1048576 | tf_op jit(solution)/shard_map/all_to_all | solution.py:42
  96.4 0.0 copy-done
  96.4 0.1 constant_dynamic-slice_fusion
  96.5 0.1 copy.14
  96.5 32.8 %all-to-all-done.2 = f32[32,2,192,8]{2,3,1,0:T(8,128)} async-done(((f32[32,2,192,8]{2,3,1,0:T(8,128)}), f32[32,2,192,8]{2,3,1,0:T(8,128)}, u32[]{:S(2)}, u32[]{:S(2)}) %all-to-all-start.2) | async-done | bytes 393248 | tf_op jit(solution)/shard_map/all_to_all | solution.py:42
  129.3 1.1 reduce_sum.9
  130.4 0.1 broadcast_in_dim.2
  130.5 39.3 %all_to_all.22 = f32[32,2,192,8]{2,3,1,0:T(8,128)S(1)} all-to-all(f32[32,2,192,8]{2,3,1,0:T(8,128)S(1)} %broadcast_in_dim.2), channel_id=1, replica_groups=mesh['row_0'=4,'row_1'=4,'mode'=32] {'mode'}, dimensions={0} | all-to-all | bytes 786432 | tf_op jit(solution)/shard_map/all_to_all | solution.py:48
  169.8 2.7 %fusion.20 = f32[192,1536]{1,0:T(8,128)S(1)} fusion(f32[1536,256]{1,0:T(8,128)S(1)} %bitcast.53, f32[2,192,32,8]{1,3,0,2:T(8,128)S(1)} %bitcast.60), kind=kOutput, calls=%fused_computation.22 | convolution fusion | flops 905969664 | bytes 3014656 | tf_op jit(solution)/shard_map/dot_general | solution.py:63
  172.5 2.7 %fusion.21 = f32[192,1536]{1,0:T(8,128)S(1)} fusion(f32[1536,256]{1,0:T(8,128)S(1)} %bitcast.54, f32[2,192,32,8]{1,3,0,2:T(8,128)S(1)} %bitcast.61), kind=kOutput, calls=%fused_computation.23 | convolution fusion | flops 905969664 | bytes 3014656 | tf_op jit(solution)/shard_map/dot_general | solution.py:63
  175.1 2.7 %fusion = f32[1,192,1536]{2,1,0:T(8,128)S(1)} fusion(f32[192,1536]{1,0:T(8,128)S(1)} %fusion.20, f32[1536,256]{1,0:T(8,128)S(1)} %bitcast.57, f32[2,192,32,8]{1,3,0,2:T(8,128)S(1)} %bitcast.62), kind=kOutput, calls=%fused_computation.2 | convolution fusion | flops 906264576 | bytes 4194304 | tf_op jit(solution)/shard_map/dot_general | solution.py:63
  177.8 2.7 %fusion.1 = f32[1,192,1536]{2,1,0:T(8,128)S(1)} fusion(f32[192,1536]{1,0:T(8,128)S(1)} %fusion.21, f32[1536,256]{1,0:T(8,128)S(1)} %bitcast.58, f32[2,192,32,8]{1,3,0,2:T(8,128)S(1)} %bitcast.63), kind=kOutput, calls=%fused_computation.3 | convolution fusion | flops 906264576 | bytes 4194304 | tf_op jit(solution)/shard_map/dot_general | solution.py:63
  180.5 1.6 pad_maximum_fusion
  (2 shorter events, 0.0 us)
Async XLA Ops:
  0.0 96.4 %copy-start = (f32[192,256]{1,0:T(8,128)S(1)}, f32[192,256]{1,0:T(8,128)}, u32[]{:S(2)}) copy-start(f32[192,256]{1,0:T(8,128)} %param.5) | copy-start | bytes 589828
  66.2 1.7 copy-start.1
  80.8 48.5 %all-to-all-start.2 = ((f32[32,2,192,8]{2,3,1,0:T(8,128)}), f32[32,2,192,8]{2,3,1,0:T(8,128)}, u32[]{:S(2)}, u32[]{:S(2)}) async-start(f32[32,2,192,8]{2,3,1,0:T(8,128)} %copy.10), calls=%async_computation.2 | async-start | bytes 1048576 | tf_op jit(solution)/shard_map/all_to_all | solution.py:42
